TPU v7x, 32 devices: a whole 2x2x4 slice. The times are simulated.
32 devices in a mesh: groups: 2 (over x), row: 16 (over z, y, core).
Axes of the slice: x: 2, y: 2, z: 4, core: 2. Of those that a mesh axis runs over, the one named last changes fastest.
Arguments:
- coupling: bfloat16 [32768, 896], P(('groups', 'row')), parts along dimension 0, may hold values from -6 to 6
- column_block: bfloat16 [32768, 1536], P(('groups', 'row')), parts along dimension 0, may hold values from -6 to 6
- pivot_inverse: bfloat16 [3072, 1536], P(('groups', 'row')), parts along dimension 0, may hold values from -0.15625 to 0.15625
- row_panel: bfloat16 [1536, 1792], P(None, ('groups', 'row')), parts along dimension 1, may hold values from -0.15625 to 0.15625
Outputs:
- lower_panel: bfloat16 [32768, 1536], P(('groups', 'row')), parts along dimension 0
- schur: bfloat16 [32768, 896], P(('groups', 'row')), parts along dimension 0
There are 2 independent parts, one for each index of `groups`. A program takes and returns all parts, laid end to end along the dimension named above; each array names one. Nothing has to cross between parts.
All inputs are finite; a program needn't handle non-finite values.
Results may differ from a plain program's by a relative error of at most 0.0039.
Values may be sent and summed in bfloat16 or wider, within the bound.
No kernel may reach another device: no remote copies, remote signals or barrier semaphores. Data moves between devices by JAX's collectives and lax.ppermute only.
A program may use at most 64 MiB of HBM per device.

v0:
```python
import jax
import jax.numpy as jnp
from jax import lax
from jax.sharding import PartitionSpec as P


def on_device(coupling, column_block, pivot_inverse, row_panel):
    whole_inverse = lax.all_gather(pivot_inverse, "row", axis=0, tiled=True)
    lower_panel = jnp.dot(column_block, whole_inverse, preferred_element_type=jnp.float32).astype(
        jnp.bfloat16
    )
    product = jnp.dot(
        lower_panel,
        lax.all_gather(row_panel, "row", axis=1, tiled=True),
        preferred_element_type=jnp.float32,
    )
    schur = (coupling.astype(jnp.float32) - product).astype(jnp.bfloat16)
    return (lower_panel, schur)


def solution(mesh):
    placed = (
        P(("groups", "row"), None),
        P(("groups", "row"), None),
        P(("groups", "row"), None),
        P(None, ("groups", "row")),
    )
    return jax.shard_map(
        on_device,
        mesh=mesh,
        in_specs=placed,
        out_specs=(P(("groups", "row"), None), P(("groups", "row"), None)),
        check_vma=False,
    )
```

profile of v0, /device:TPU:0, one launch (start us, length us, event | category | flops | bytes accessed | tf_op | source)
XLA Modules:
  0.0 125.8 jit_solution(16534755584395549889)
XLA Ops:
  7.2 0.0 copy-start
  7.2 0.0 all-gather.3.cloned.1.call-start
  7.2 0.7 all-gather.3.cloned.1.call-update
  7.9 0.0 all-gather.5.cloned.1.call-start
  8.0 0.7 all-gather.5.cloned.1.call-update
  8.7 57.8 %all-gather.3.cloned.1.call-done = bf16[1536,1536]{1,0:T(8,128)(2,1)} async-done(((bf16[96,1536]{1,0:T(8,128)(2,1)}), bf16[1536,1536]{1,0:T(8,128)(2,1)}) %all-gather.3.cloned.1.call-update) | async-done | bytes 4718608 | tf_op jit(solution)/shard_map/all_gather | solution.py:8
  66.4 0.0 copy-done
  66.4 8.7 %convolution_convert_fusion = bf16[1024,1536]{1,0:T(8,128)(2,1)} fusion(bf16[1024,1536]{1,0:T(8,128)(2,1)S(1)} %copy-done, bf16[1536,1536]{1,0:T(8,128)(2,1)} %all-gather.3.cloned.1.call-done), kind=kOutput, calls=%fused_computation | convolution fusion | flops 4833411072 | bytes 11010048 | tf_op jit(solution)/shard_map/dot_general | solution.py:9
  75.1 35.9 %all-gather.5.cloned.1.call-done = bf16[1536,896]{0,1:T(8,128)(2,1)} async-done(((bf16[1536,56]{0,1:T(8,128)(2,1)}), bf16[1536,896]{0,1:T(8,128)(2,1)}) %all-gather.5.cloned.1.call-update) | async-done | bytes 2752528 | tf_op jit(solution)/shard_map/all_gather | solution.py:14
  111.0 7.9 %subtract_convert_fusion = bf16[1024,896]{1,0:T(8,128)(2,1)} fusion(bf16[1024,896]{1,0:T(8,128)(2,1)} %param.4, bf16[1024,1536]{1,0:T(8,128)(2,1)} %convolution_convert_fusion, bf16[1536,896]{0,1:T(8,128)(2,1)} %all-gather.5.cloned.1.call-done), kind=kOutput, calls=%fused_computation.1 | convolution fusion | flops 2821324800 | bytes 9568256 | tf_op jit(solution)/shard_map/dot_general | solution.py:12
Async XLA Ops:
  7.2 59.3 %copy-start = (bf16[1024,1536]{1,0:T(8,128)(2,1)S(1)}, bf16[1024,1536]{1,0:T(8,128)(2,1)}, u32[]{:S(2)}) copy-start(bf16[1024,1536]{1,0:T(8,128)(2,1)} %param.5) | copy-start | bytes 9437188
  7.2 59.2 %all-gather.3.cloned.1.call-start = ((), (), s32[]{:S(2)}) async-start(), calls=%async_computation | async-start | bytes 5013504 | tf_op jit(solution)/shard_map/all_gather | solution.py:8
  7.9 103.1 %all-gather.5.cloned.1.call-start = ((), (), s32[]{:S(2)}) async-start(), calls=%async_computation.1 | async-start | bytes 2924544 | tf_op jit(solution)/shard_map/all_gather | solution.py:14
Sparse Core Ops, SparseCore 0:
  10.3 56.0 all-gather.2
  68.7 42.2 all-gather.4
where the time goes:
time: 126 us
  waiting for transfers between devices  95 us (75%)
  matrix products  16.6 us (13%)
  between operations  14 us (11%)
    all_gather x1, waiting for transfers between devices, on_device(): whole_inverse = lax.all_gather(pivot_inverse, 'row', axis=0, tiled=True)  57.8 us
    all_gather x1, waiting for transfers between devices, on_device(): lax.all_gather(row_panel, 'row', axis=1, tiled=True)  35.9 us
    dot_general x1, matrix products, on_device(): jnp.dot(column_block, whole_inverse, preferred_element_type=jnp.float32)  8.69 us
    dot_general x1, matrix products, on_device(): jnp.dot(lower_panel, lax.all_gather(row_panel, 'row', axis=1, tiled=True)...  7.92 us
  transfers between devices with their start and end apart: 2, of which 2 were waited for; matrix products, arithmetic and copies ran while one was open for 7% of the time, Pallas kernels for 0%

commit v1 on v0

--- a/solution.py
+++ b/solution.py
@@ -2,6 +2,27 @@
 import jax.numpy as jnp
 from jax import lax
 from jax.sharding import PartitionSpec as P
+
+
+def gather_around(array, axis, dim):
+    size, mine, width = (lax.axis_size(axis), lax.axis_index(axis), array.shape[dim])
+    right = [(i, (i + 1) % size) for i in range(size)]
+    left = [(i, (i - 1) % size) for i in range(size)]
+    whole = jnp.zeros((*array.shape[:dim], size * width, *array.shape[dim + 1 :]), array.dtype)
+    whole = lax.dynamic_update_slice_in_dim(whole, array, mine * width, axis=dim)
+    from_left = from_right = array
+    halfway = size // 2
+    for lap in range(1, halfway + 1):
+        from_left = lax.ppermute(from_left, axis, right)
+        whole = lax.dynamic_update_slice_in_dim(
+            whole, from_left, (mine - lap) % size * width, axis=dim
+        )
+        if lap < size - halfway:
+            from_right = lax.ppermute(from_right, axis, left)
+            whole = lax.dynamic_update_slice_in_dim(
+                whole, from_right, (mine + lap) % size * width, axis=dim
+            )
+    return whole
 
 
 def on_device(coupling, column_block, pivot_inverse, row_panel):
@@ -10,9 +31,7 @@
         jnp.bfloat16
     )
     product = jnp.dot(
-        lower_panel,
-        lax.all_gather(row_panel, "row", axis=1, tiled=True),
-        preferred_element_type=jnp.float32,
+        lower_panel, gather_around(row_panel, "row", 1), preferred_element_type=jnp.float32
     )
     schur = (coupling.astype(jnp.float32) - product).astype(jnp.bfloat16)
     return (lower_panel, schur)

time: 126 us -> 101 us (0.80)
  waiting for transfers between devices: 95 us -> 25.1 us
  starting transfers between devices: 0.08 us -> 33.3 us
  local copies, waits for them, and re-layouts: 0.01 us -> 13.6 us
  matrix products: 16.6 us -> 15.2 us
    all_gather x1, waiting for transfers between devices: 57.8 us -> 0.01 us  [on_device(): whole_inverse = lax.all_gather(pivot_inverse, 'row', axis=0, tiled=True)]
    all_gather x1 -> x0, waiting for transfers between devices: 35.9 us -> none  [on_device(): lax.all_gather(row_panel, 'row', axis=1, tiled=True)]
    ppermute x0 -> x15, starting transfers between devices: none -> 33.3 us  [the longest x7 32.7 us: gather_around(): from_right = lax.ppermute(from_right, axis, left)]
    ppermute x0 -> x15, waiting for transfers between devices: none -> 24.4 us  [the longest x7 14.7 us: gather_around(): from_right = lax.ppermute(from_right, axis, left)]
    dynamic_update_slice x0 -> x16, local copies, waits for them, and re-layouts: none -> 11.8 us  [the longest x8 6.35 us: gather_around(): lax.dynamic_update_slice_in_dim(whole, from_left, (mine - lap) % size * w...]
    broadcast_in_dim x0 -> x1, local copies, waits for them, and re-layouts: none -> 1.74 us  [gather_around(): jnp.zeros((*array.shape[:dim], size * width, *array.shape[dim + 1:]), arr...]
  transfers between devices with their start and end apart: 2 -> 16, of which waited for: 2 -> 13; matrix products, arithmetic and copies ran while one was open for 7% -> 13% of each run, Pallas kernels for 0% -> 0%
where the time goes in v1:
time: 101 us
  starting transfers between devices  33.3 us (33%)
  waiting for transfers between devices  25.1 us (25%)
  matrix products  15.2 us (15%)
  between operations  14.1 us (14%)
  local copies, waits for them, and re-layouts  13.6 us (13%)
    ppermute x7, starting transfers between devices, gather_around(): from_right = lax.ppermute(from_right, axis, left)  32.7 us
    ppermute x7, waiting for transfers between devices, gather_around(): from_right = lax.ppermute(from_right, axis, left)  14.7 us
    ppermute x8, waiting for transfers between devices, gather_around(): from_left = lax.ppermute(from_left, axis, right)  9.68 us
    dot_general x1, matrix products, on_device(): jnp.dot(column_block, whole_inverse, preferred_element_type=jnp.float32)  7.7 us
    dot_general x1, matrix products, on_device(): jnp.dot(lower_panel, gather_around(row_panel, 'row', 1), preferred_elemen...  7.52 us
    dynamic_update_slice x8, local copies, waits for them, and re-layouts, gather_around(): lax.dynamic_update_slice_in_dim(whole, from_left, (mine - lap) % size * w...  6.35 us
    dynamic_update_slice x7, local copies, waits for them, and re-layouts, gather_around(): lax.dynamic_update_slice_in_dim(whole, from_right, (mine + lap) % size *...  4.77 us
  transfers between devices with their start and end apart: 16, of which 13 were waited for; matrix products, arithmetic and copies ran while one was open for 13% of the time, Pallas kernels for 0%

profile of v1, /device:TPU:0, one launch (start us, length us, event | category | flops | bytes accessed | tf_op | source)
XLA Modules:
  0.0 101.3 jit_solution(16633424082366613654)
XLA Ops:
  8.4 5.1 %collective-permute-start.1 = (bf16[1536,56]{0,1:T(8,128)(2,1)}, bf16[1536,56]{0,1:T(8,128)(2,1)S(1)}, u32[]{:S(2)}, u32[]{:S(2)}) collective-permute-start(bf16[1536,56]{0,1:T(8,128)(2,1)} %param.7), channel_id=1, source_target_pairs={{0,15},{1,0},{2,1},{3,2},{4,3},{5,4},{6,5},{7,6},{8,7},{9,8},{10,9... | collective-permute-start | bytes 516104 | tf_op jit(solution)/shard_map/ppermute | solution.py:21
  13.5 1.7 %broadcast_in_dim.3 = bf16[1536,896]{0,1:T(8,128)(2,1)} broadcast(bf16[]{:T(256)} %constant.89.clone.1), dimensions={} | broadcast | bytes 2752514 | tf_op jit(solution)/shard_map/broadcast_in_dim | solution.py:11
  15.2 0.7 constant_dynamic-update-slice_fusion.15
  15.9 1.0 %collective-permute-done = bf16[1536,56]{0,1:T(8,128)(2,1)} collective-permute-done((bf16[1536,56]{0,1:T(8,128)(2,1)}, bf16[1536,56]{0,1:T(8,128)(2,1)}, u32[]{:S(2)}, u32[]{:S(2)}) %collective-permute-start) | collective-permute-done | bytes 172064 | tf_op jit(solution)/shard_map/ppermute | solution.py:16
  16.9 4.4 %collective-permute-start.3 = (bf16[1536,56]{0,1:T(8,128)(2,1)S(1)}, bf16[1536,56]{0,1:T(8,128)(2,1)S(1)}, u32[]{:S(2)}, u32[]{:S(2)}) collective-permute-start(bf16[1536,56]{0,1:T(8,128)(2,1)S(1)} %collective-permute-done.1), channel_id=1, source_target_pairs={{0,15},{1,0},{2,1},{3,2},{4,3},{5,4},{6,5},{7,6},{8,7},{9,8},{10,9... | collective-permute-start | bytes 516104 | tf_op jit(solution)/shard_map/ppermute | solution.py:21
  21.4 1.6 %constant_dynamic-update-slice_fusion.14 = bf16[1536,896]{0,1:T(8,128)(2,1)} fusion(bf16[1536,896]{0,1:T(8,128)(2,1)} %constant_dynamic-update-slice_fusion.15, bf16[1536,56]{0,1:T(8,128)(2,1)} %collective-permute-done, s32[]{:T(128)S(6)} %select_n.113), kind=kLoop, calls=%fused_computation.16 | loop fusion | bytes 344068 | tf_op jit(solution)/shard_map/dynamic_update_slice | solution.py:17
  23.7 1.1 %collective-permute-done.2 = bf16[1536,56]{0,1:T(8,128)(2,1)S(1)} collective-permute-done((bf16[1536,56]{0,1:T(8,128)(2,1)}, bf16[1536,56]{0,1:T(8,128)(2,1)S(1)}, u32[]{:S(2)}, u32[]{:S(2)}) %collective-permute-start.2) | collective-permute-done | bytes 172064 | tf_op jit(solution)/shard_map/ppermute | solution.py:16
  24.8 2.1 %collective-permute-done.3 = bf16[1536,56]{0,1:T(8,128)(2,1)S(1)} collective-permute-done((bf16[1536,56]{0,1:T(8,128)(2,1)S(1)}, bf16[1536,56]{0,1:T(8,128)(2,1)S(1)}, u32[]{:S(2)}, u32[]{:S(2)}) %collective-permute-start.3) | collective-permute-done | bytes 172064 | tf_op jit(solution)/shard_map/ppermute | solution.py:21
  26.9 4.6 %collective-permute-start.5 = (bf16[1536,56]{0,1:T(8,128)(2,1)S(1)}, bf16[1536,56]{0,1:T(8,128)(2,1)S(1)}, u32[]{:S(2)}, u32[]{:S(2)}) collective-permute-start(bf16[1536,56]{0,1:T(8,128)(2,1)S(1)} %collective-permute-done.3), channel_id=1, source_target_pairs={{0,15},{1,0},{2,1},{3,2},{4,3},{5,4},{6,5},{7,6},{8,7},{9,8},{10,9... | collective-permute-start | bytes 516104 | tf_op jit(solution)/shard_map/ppermute | solution.py:21
  33.6 1.9 %collective-permute-done.5 = bf16[1536,56]{0,1:T(8,128)(2,1)S(1)} collective-permute-done((bf16[1536,56]{0,1:T(8,128)(2,1)S(1)}, bf16[1536,56]{0,1:T(8,128)(2,1)S(1)}, u32[]{:S(2)}, u32[]{:S(2)}) %collective-permute-start.5) | collective-permute-done | bytes 172064 | tf_op jit(solution)/shard_map/ppermute | solution.py:21
  35.5 4.6 %collective-permute-start.7 = (bf16[1536,56]{0,1:T(8,128)(2,1)S(1)}, bf16[1536,56]{0,1:T(8,128)(2,1)S(1)}, u32[]{:S(2)}, u32[]{:S(2)}) collective-permute-start(bf16[1536,56]{0,1:T(8,128)(2,1)S(1)} %collective-permute-done.5), channel_id=1, source_target_pairs={{0,15},{1,0},{2,1},{3,2},{4,3},{5,4},{6,5},{7,6},{8,7},{9,8},{10,9... | collective-permute-start | bytes 516104 | tf_op jit(solution)/shard_map/ppermute | solution.py:21
  41.5 1.6 %collective-permute-done.7 = bf16[1536,56]{0,1:T(8,128)(2,1)S(1)} collective-permute-done((bf16[1536,56]{0,1:T(8,128)(2,1)S(1)}, bf16[1536,56]{0,1:T(8,128)(2,1)S(1)}, u32[]{:S(2)}, u32[]{:S(2)}) %collective-permute-start.7) | collective-permute-done | bytes 172064 | tf_op jit(solution)/shard_map/ppermute | solution.py:21
  43.0 4.6 %collective-permute-start.9 = (bf16[1536,56]{0,1:T(8,128)(2,1)S(1)}, bf16[1536,56]{0,1:T(8,128)(2,1)S(1)}, u32[]{:S(2)}, u32[]{:S(2)}) collective-permute-start(bf16[1536,56]{0,1:T(8,128)(2,1)S(1)} %collective-permute-done.7), channel_id=1, source_target_pairs={{0,15},{1,0},{2,1},{3,2},{4,3},{5,4},{6,5},{7,6},{8,7},{9,8},{10,9... | collective-permute-start | bytes 516104 | tf_op jit(solution)/shard_map/ppermute | solution.py:21
  47.7 0.7 constant_dynamic-update-slice_fusion.8
  48.3 0.7 constant_dynamic-update-slice_fusion.7
  49.0 0.9 collective-permute-done.8
  49.9 4.1 %collective-permute-done.9 = bf16[1536,56]{0,1:T(8,128)(2,1)S(1)} collective-permute-done((bf16[1536,56]{0,1:T(8,128)(2,1)S(1)}, bf16[1536,56]{0,1:T(8,128)(2,1)S(1)}, u32[]{:S(2)}, u32[]{:S(2)}) %collective-permute-start.9) | collective-permute-done | bytes 172064 | tf_op jit(solution)/shard_map/ppermute | solution.py:21
  54.0 4.6 %collective-permute-start.11 = (bf16[1536,56]{0,1:T(8,128)(2,1)S(1)}, bf16[1536,56]{0,1:T(8,128)(2,1)S(1)}, u32[]{:S(2)}, u32[]{:S(2)}) collective-permute-start(bf16[1536,56]{0,1:T(8,128)(2,1)S(1)} %collective-permute-done.9), channel_id=1, source_target_pairs={{0,15},{1,0},{2,1},{3,2},{4,3},{5,4},{6,5},{7,6},{8,7},{9,8},{10,9... | collective-permute-start | bytes 516104 | tf_op jit(solution)/shard_map/ppermute | solution.py:21
  60.5 1.1 %collective-permute-done.11 = bf16[1536,56]{0,1:T(8,128)(2,1)S(1)} collective-permute-done((bf16[1536,56]{0,1:T(8,128)(2,1)S(1)}, bf16[1536,56]{0,1:T(8,128)(2,1)S(1)}, u32[]{:S(2)}, u32[]{:S(2)}) %collective-permute-start.11) | collective-permute-done | bytes 172064 | tf_op jit(solution)/shard_map/ppermute | solution.py:21
  61.6 4.8 %collective-permute-start.13 = (bf16[1536,56]{0,1:T(8,128)(2,1)S(1)}, bf16[1536,56]{0,1:T(8,128)(2,1)S(1)}, u32[]{:S(2)}, u32[]{:S(2)}) collective-permute-start(bf16[1536,56]{0,1:T(8,128)(2,1)S(1)} %collective-permute-done.11), channel_id=1, source_target_pairs={{0,15},{1,0},{2,1},{3,2},{4,3},{5,4},{6,5},{7,6},{8,7},{9,8},{10,9... | collective-permute-start | bytes 516104 | tf_op jit(solution)/shard_map/ppermute | solution.py:21
  68.7 3.9 %collective-permute-done.13 = bf16[1536,56]{0,1:T(8,128)(2,1)S(1)} collective-permute-done((bf16[1536,56]{0,1:T(8,128)(2,1)S(1)}, bf16[1536,56]{0,1:T(8,128)(2,1)S(1)}, u32[]{:S(2)}, u32[]{:S(2)}) %collective-permute-start.13) | collective-permute-done | bytes 172064 | tf_op jit(solution)/shard_map/ppermute | solution.py:21
  73.3 5.2 %collective-permute-done.14 = bf16[1536,56]{0,1:T(8,128)(2,1)S(1)} collective-permute-done((bf16[1536,56]{0,1:T(8,128)(2,1)S(1)}, bf16[1536,56]{0,1:T(8,128)(2,1)S(1)}, u32[]{:S(2)}, u32[]{:S(2)}) %collective-permute-start.14) | collective-permute-done | bytes 172064 | tf_op jit(solution)/shard_map/ppermute | solution.py:16
  79.2 7.7 %convolution_convert_fusion = bf16[1024,1536]{1,0:T(8,128)(2,1)S(1)} fusion(bf16[1024,1536]{1,0:T(8,128)(2,1)S(1)} %copy-done, bf16[1536,1536]{1,0:T(8,128)(2,1)} %all-gather.2.cloned.1.call-done), kind=kOutput, calls=%fused_computation | convolution fusion | flops 4833411072 | bytes 11010048 | tf_op jit(solution)/shard_map/dot_general | solution.py:30
  86.9 7.5 %subtract_convert_fusion = bf16[1024,896]{1,0:T(8,128)(2,1)} fusion(bf16[1024,896]{1,0:T(8,128)(2,1)S(1)} %copy-done.2, bf16[1024,1536]{1,0:T(8,128)(2,1)S(1)} %convolution_convert_fusion, bf16[1536,896]{0,1:T(8,128)(2,1)} %constant_dynamic-update-slice_fusion), kind=kOutput, calls=%fused_computation.1 | convolution fusion | flops 2821324800 | bytes 9568256 | tf_op jit(solution)/shard_map/dot_general | solution.py:33
  (36 shorter events, 10.9 us)
Async XLA Ops:
  7.2 72.0 %copy-start = (bf16[1024,1536]{1,0:T(8,128)(2,1)S(1)}, bf16[1024,1536]{1,0:T(8,128)(2,1)}, u32[]{:S(2)}) copy-start(bf16[1024,1536]{1,0:T(8,128)(2,1)} %param.5) | copy-start | bytes 9437188
  7.2 8.0 %copy-start.1 = (bf16[1536,56]{0,1:T(8,128)(2,1)S(1)}, bf16[1536,56]{0,1:T(8,128)(2,1)}, u32[]{:S(2)}) copy-start(bf16[1536,56]{0,1:T(8,128)(2,1)} %param.7) | copy-start | bytes 516100
  7.2 72.0 %all-gather.2.cloned.1.call-start = ((), (), s32[]{:S(2)}) async-start(), calls=%async_computation | async-start | bytes 5013504 | tf_op jit(solution)/shard_map/all_gather | solution.py:29
  7.9 9.0 %collective-permute-start = (bf16[1536,56]{0,1:T(8,128)(2,1)}, bf16[1536,56]{0,1:T(8,128)(2,1)}, u32[]{:S(2)}, u32[]{:S(2)}) collective-permute-start(bf16[1536,56]{0,1:T(8,128)(2,1)} %param.7), channel_id=1, source_target_pairs={{0,1},{1,2},{2,3},{3,4},{4,5},{5,6},{6,7},{7,8},{8,9},{9,10},{10,1... | collective-permute-start | bytes 516104 | tf_op jit(solution)/shard_map/ppermute | solution.py:16
  8.4 8.5 %collective-permute-start.1 = (bf16[1536,56]{0,1:T(8,128)(2,1)}, bf16[1536,56]{0,1:T(8,128)(2,1)S(1)}, u32[]{:S(2)}, u32[]{:S(2)}) collective-permute-start(bf16[1536,56]{0,1:T(8,128)(2,1)} %param.7), channel_id=1, source_target_pairs={{0,15},{1,0},{2,1},{3,2},{4,3},{5,4},{6,5},{7,6},{8,7},{9,8},{10,9... | collective-permute-start | bytes 516104 | tf_op jit(solution)/shard_map/ppermute | solution.py:21
  16.9 7.8 %collective-permute-start.2 = (bf16[1536,56]{0,1:T(8,128)(2,1)}, bf16[1536,56]{0,1:T(8,128)(2,1)S(1)}, u32[]{:S(2)}, u32[]{:S(2)}) collective-permute-start(bf16[1536,56]{0,1:T(8,128)(2,1)} %collective-permute-done), channel_id=1, source_target_pairs={{0,1},{1,2},{2,3},{3,4},{4,5},{5,6},{6,7},{7,8},{8,9},{9,10},{10,1... | collective-permute-start | bytes 516104 | tf_op jit(solution)/shard_map/ppermute | solution.py:16
  16.9 10.0 %collective-permute-start.3 = (bf16[1536,56]{0,1:T(8,128)(2,1)S(1)}, bf16[1536,56]{0,1:T(8,128)(2,1)S(1)}, u32[]{:S(2)}, u32[]{:S(2)}) collective-permute-start(bf16[1536,56]{0,1:T(8,128)(2,1)S(1)} %collective-permute-done.1), channel_id=1, source_target_pairs={{0,15},{1,0},{2,1},{3,2},{4,3},{5,4},{6,5},{7,6},{8,7},{9,8},{10,9... | collective-permute-start | bytes 516104 | tf_op jit(solution)/shard_map/ppermute | solution.py:21
  24.8 8.8 %collective-permute-start.4 = (bf16[1536,56]{0,1:T(8,128)(2,1)S(1)}, bf16[1536,56]{0,1:T(8,128)(2,1)S(1)}, u32[]{:S(2)}, u32[]{:S(2)}) collective-permute-start(bf16[1536,56]{0,1:T(8,128)(2,1)S(1)} %collective-permute-done.2), channel_id=1, source_target_pairs={{0,1},{1,2},{2,3},{3,4},{4,5},{5,6},{6,7},{7,8},{8,9},{9,10},{10,1... | collective-permute-start | bytes 516104 | tf_op jit(solution)/shard_map/ppermute | solution.py:16
  26.9 8.6 %collective-permute-start.5 = (bf16[1536,56]{0,1:T(8,128)(2,1)S(1)}, bf16[1536,56]{0,1:T(8,128)(2,1)S(1)}, u32[]{:S(2)}, u32[]{:S(2)}) collective-permute-start(bf16[1536,56]{0,1:T(8,128)(2,1)S(1)} %collective-permute-done.3), channel_id=1, source_target_pairs={{0,15},{1,0},{2,1},{3,2},{4,3},{5,4},{6,5},{7,6},{8,7},{9,8},{10,9... | collective-permute-start | bytes 516104 | tf_op jit(solution)/shard_map/ppermute | solution.py:21
  33.6 7.9 %collective-permute-start.6 = (bf16[1536,56]{0,1:T(8,128)(2,1)S(1)}, bf16[1536,56]{0,1:T(8,128)(2,1)S(1)}, u32[]{:S(2)}, u32[]{:S(2)}) collective-permute-start(bf16[1536,56]{0,1:T(8,128)(2,1)S(1)} %collective-permute-done.4), channel_id=1, source_target_pairs={{0,1},{1,2},{2,3},{3,4},{4,5},{5,6},{6,7},{7,8},{8,9},{9,10},{10,1... | collective-permute-start | bytes 516104 | tf_op jit(solution)/shard_map/ppermute | solution.py:16
  35.5 7.5 %collective-permute-start.7 = (bf16[1536,56]{0,1:T(8,128)(2,1)S(1)}, bf16[1536,56]{0,1:T(8,128)(2,1)S(1)}, u32[]{:S(2)}, u32[]{:S(2)}) collective-permute-start(bf16[1536,56]{0,1:T(8,128)(2,1)S(1)} %collective-permute-done.5), channel_id=1, source_target_pairs={{0,15},{1,0},{2,1},{3,2},{4,3},{5,4},{6,5},{7,6},{8,7},{9,8},{10,9... | collective-permute-start | bytes 516104 | tf_op jit(solution)/shard_map/ppermute | solution.py:21
  41.5 8.5 %collective-permute-start.8 = (bf16[1536,56]{0,1:T(8,128)(2,1)S(1)}, bf16[1536,56]{0,1:T(8,128)(2,1)S(1)}, u32[]{:S(2)}, u32[]{:S(2)}) collective-permute-start(bf16[1536,56]{0,1:T(8,128)(2,1)S(1)} %collective-permute-done.6), channel_id=1, source_target_pairs={{0,1},{1,2},{2,3},{3,4},{4,5},{5,6},{6,7},{7,8},{8,9},{9,10},{10,1... | collective-permute-start | bytes 516104 | tf_op jit(solution)/shard_map/ppermute | solution.py:16
  43.0 11.0 %collective-permute-start.9 = (bf16[1536,56]{0,1:T(8,128)(2,1)S(1)}, bf16[1536,56]{0,1:T(8,128)(2,1)S(1)}, u32[]{:S(2)}, u32[]{:S(2)}) collective-permute-start(bf16[1536,56]{0,1:T(8,128)(2,1)S(1)} %collective-permute-done.7), channel_id=1, source_target_pairs={{0,15},{1,0},{2,1},{3,2},{4,3},{5,4},{6,5},{7,6},{8,7},{9,8},{10,9... | collective-permute-start | bytes 516104 | tf_op jit(solution)/shard_map/ppermute | solution.py:21
  49.9 10.6 %collective-permute-start.10 = (bf16[1536,56]{0,1:T(8,128)(2,1)S(1)}, bf16[1536,56]{0,1:T(8,128)(2,1)S(1)}, u32[]{:S(2)}, u32[]{:S(2)}) collective-permute-start(bf16[1536,56]{0,1:T(8,128)(2,1)S(1)} %collective-permute-done.8), channel_id=1, source_target_pairs={{0,1},{1,2},{2,3},{3,4},{4,5},{5,6},{6,7},{7,8},{8,9},{9,10},{10,1... | collective-permute-start | bytes 516104 | tf_op jit(solution)/shard_map/ppermute | solution.py:16
  54.0 7.5 %collective-permute-start.11 = (bf16[1536,56]{0,1:T(8,128)(2,1)S(1)}, bf16[1536,56]{0,1:T(8,128)(2,1)S(1)}, u32[]{:S(2)}, u32[]{:S(2)}) collective-permute-start(bf16[1536,56]{0,1:T(8,128)(2,1)S(1)} %collective-permute-done.9), channel_id=1, source_target_pairs={{0,15},{1,0},{2,1},{3,2},{4,3},{5,4},{6,5},{7,6},{8,7},{9,8},{10,9... | collective-permute-start | bytes 516104 | tf_op jit(solution)/shard_map/ppermute | solution.py:21
  60.5 7.5 %collective-permute-start.12 = (bf16[1536,56]{0,1:T(8,128)(2,1)S(1)}, bf16[1536,56]{0,1:T(8,128)(2,1)S(1)}, u32[]{:S(2)}, u32[]{:S(2)}) collective-permute-start(bf16[1536,56]{0,1:T(8,128)(2,1)S(1)} %collective-permute-done.10), channel_id=1, source_target_pairs={{0,1},{1,2},{2,3},{3,4},{4,5},{5,6},{6,7},{7,8},{8,9},{9,10},{10,1... | collective-permute-start | bytes 516104 | tf_op jit(solution)/shard_map/ppermute | solution.py:16
  61.6 11.0 %collective-permute-start.13 = (bf16[1536,56]{0,1:T(8,128)(2,1)S(1)}, bf16[1536,56]{0,1:T(8,128)(2,1)S(1)}, u32[]{:S(2)}, u32[]{:S(2)}) collective-permute-start(bf16[1536,56]{0,1:T(8,128)(2,1)S(1)} %collective-permute-done.11), channel_id=1, source_target_pairs={{0,15},{1,0},{2,1},{3,2},{4,3},{5,4},{6,5},{7,6},{8,7},{9,8},{10,9... | collective-permute-start | bytes 516104 | tf_op jit(solution)/shard_map/ppermute | solution.py:21
  68.0 10.5 %collective-permute-start.14 = (bf16[1536,56]{0,1:T(8,128)(2,1)S(1)}, bf16[1536,56]{0,1:T(8,128)(2,1)S(1)}, u32[]{:S(2)}, u32[]{:S(2)}) collective-permute-start(bf16[1536,56]{0,1:T(8,128)(2,1)S(1)} %collective-permute-done.12), channel_id=1, source_target_pairs={{0,1},{1,2},{2,3},{3,4},{4,5},{5,6},{6,7},{7,8},{8,9},{9,10},{10,1... | collective-permute-start | bytes 516104 | tf_op jit(solution)/shard_map/ppermute | solution.py:16
  79.2 7.7 %copy-start.2 = (bf16[1024,896]{1,0:T(8,128)(2,1)S(1)}, bf16[1024,896]{1,0:T(8,128)(2,1)}, u32[]{:S(2)}) copy-start(bf16[1024,896]{1,0:T(8,128)(2,1)} %param.4) | copy-start | bytes 5505028
  86.9 7.5 %copy-start.3 = (bf16[1024,1536]{1,0:T(8,128)(2,1)}, bf16[1024,1536]{1,0:T(8,128)(2,1)S(1)}, u32[]{:S(2)}) copy-start(bf16[1024,1536]{1,0:T(8,128)(2,1)S(1)} %convolution_convert_fusion) | copy-start | bytes 9437188
Sparse Core Ops, SparseCore 0:
  10.3 67.4 all-gather.1
